TPU v7x, 32 devices: a whole 2x2x4 slice. The times are simulated.
32 devices in a mesh: dp: 2 (over x), expert: 16 (over z, y, core).
Axes of the slice: x: 2, y: 2, z: 4, core: 2. Of those that a mesh axis runs over, the one named last changes fastest.
Arguments:
- tokens: bfloat16 [512, 4096], P('expert'), may hold values from -6 to 6
- expert_ids: int32 [512, 8], P('expert'), may hold values from 0 to 15, all different within a row; in each aligned block of 32 rows (0 to 31, 32 to 63, ...) at most 24 rows name the same one
- gate_ints: int32 [512, 8], P('expert'), may hold values from 1 to 1024
- w_gate: bfloat16 [16, 4096, 1536], P('expert', None, 'dp'), may hold values from -0.09375 to 0.09375
- w_up: bfloat16 [16, 4096, 1536], P('expert', None, 'dp'), may hold values from -0.09375 to 0.09375
- w_down: bfloat16 [16, 1536, 4096], P('expert', 'dp'), may hold values from -0.15625 to 0.15625
Outputs:
- mixed: bfloat16 [512, 4096], P('expert')
Inputs may be any that keep to these rules, and one draw needn't show every extreme that they name: `expert_ids`: within the rows of one device each expert is named at most 24 times, and each row names 8 different experts.
All inputs are finite; a program needn't handle non-finite values.
Results may differ from a plain program's by a relative error of at most 0.017.
Values may be sent and summed in bfloat16 or wider, within the bound.
A program may use at most 64 MiB of HBM per device.

v0:
```python
import jax
import jax.numpy as jnp
from jax import lax
from jax.sharding import PartitionSpec as P


def dispatch_form(tokens, expert_ids, gate_ints, w_gate, w_up, w_down):
    tok_rows = tokens.shape[0]
    top_count = expert_ids.shape[1]
    feature = tokens.shape[1]
    groups = lax.axis_size("expert")
    capacity = min(tok_rows, max(2, 3 * tok_rows * top_count // (2 * groups)))
    pairs = tok_rows * top_count
    flat_ids = expert_ids.reshape(pairs)
    onehot = (flat_ids[:, None] == jnp.arange(groups, dtype=jnp.int32)[None, :]).astype(jnp.int32)
    before = jnp.cumsum(onehot, axis=0) - onehot
    slot = jnp.sum(before * onehot, axis=1)
    target = flat_ids * capacity + slot
    select = (jnp.arange(groups * capacity, dtype=jnp.int32)[:, None] == target[None, :]).astype(
        jnp.bfloat16
    )
    owner = (
        (jnp.arange(pairs, dtype=jnp.int32) // top_count)[:, None]
        == jnp.arange(tok_rows, dtype=jnp.int32)[None, :]
    ).astype(jnp.bfloat16)
    placing = jnp.dot(select, owner, preferred_element_type=jnp.float32).astype(jnp.bfloat16)
    outgoing = jnp.dot(placing, tokens, preferred_element_type=jnp.float32).astype(jnp.bfloat16)
    arrived = lax.all_to_all(
        outgoing.reshape(groups, capacity, feature),
        "expert",
        split_axis=0,
        concat_axis=0,
        tiled=True,
    )
    rows = arrived.reshape(groups * capacity, feature)
    gate = jnp.dot(rows, w_gate[0], preferred_element_type=jnp.float32)
    up = jnp.dot(rows, w_up[0], preferred_element_type=jnp.float32)
    hidden = (jax.nn.silu(gate) * up).astype(jnp.bfloat16)
    partial_value = jnp.dot(hidden, w_down[0], preferred_element_type=jnp.float32).astype(
        jnp.bfloat16
    )
    back = lax.all_to_all(
        partial_value.reshape(groups, capacity, feature),
        "expert",
        split_axis=0,
        concat_axis=0,
        tiled=True,
    )
    back_rows = back.reshape(groups * capacity, feature)
    weights = (gate_ints.astype(jnp.float32) / 1024.0)[:, :, None]
    picked = (
        jnp.take(back_rows, target, axis=0)
        .reshape(tok_rows, top_count, feature)
        .astype(jnp.float32)
    )
    local_mix = jnp.sum(weights * picked, axis=1)
    mixed = lax.psum(local_mix.astype(jnp.bfloat16), "dp")
    return mixed


def dense_form(tokens, expert_ids, gate_ints, w_gate, w_up, w_down):
    groups = lax.axis_size("expert")
    me = lax.axis_index("expert")
    chosen = expert_ids[:, :, None] == jnp.arange(groups, dtype=jnp.int32)[None, None, :]
    coef = jnp.sum(jnp.where(chosen, gate_ints[:, :, None], 0), axis=1).astype(jnp.float32) / 1024.0
    rows = lax.all_gather(tokens, "expert", axis=0, tiled=True)
    coefs = lax.all_gather(coef, "expert", axis=0, tiled=True)
    mine = lax.dynamic_slice_in_dim(coefs, me, 1, axis=1)
    gate = jnp.dot(rows, w_gate[0], preferred_element_type=jnp.float32)
    up = jnp.dot(rows, w_up[0], preferred_element_type=jnp.float32)
    hidden = (jax.nn.silu(gate) * up).astype(jnp.bfloat16)
    part = mine * jnp.dot(hidden, w_down[0], preferred_element_type=jnp.float32)
    local = lax.psum_scatter(part.astype(jnp.bfloat16), "expert", scatter_dimension=0, tiled=True)
    return lax.psum(local, "dp")


def on_device(tokens, expert_ids, *rest):
    tok_rows, top_count = expert_ids.shape
    groups = lax.axis_size("expert")
    capacity = min(tok_rows, max(2, 3 * tok_rows * top_count // (2 * groups)))
    form = dense_form if tok_rows <= 2 * capacity else dispatch_form
    return form(tokens, expert_ids, *rest)


def solution(mesh):
    return jax.shard_map(
        on_device,
        mesh=mesh,
        in_specs=(
            P("expert", None),
            P("expert", None),
            P("expert", None),
            P("expert", None, "dp"),
            P("expert", None, "dp"),
            P("expert", "dp", None),
        ),
        out_specs=P("expert", None),
        check_vma=False,
    )
```

profile of v0, /device:TPU:0, one launch (start us, length us, event | category | flops | bytes accessed | tf_op | source)
XLA Modules:
  0.0 190.7 jit_solution(241557817520303641)
XLA Ops:
  6.5 0.0 all-gather.3.cloned.1.call-start
  6.5 0.7 all-gather.3.cloned.1.call-update
  7.3 0.0 reduce-scatter.2.cloned.1.call-start
  7.3 0.7 select_reduce_fusion
  8.0 23.6 %all-gather = f32[16,32,16]{1,2,0:T(8,128)S(1)} all-gather(f32[1,32,16]{1,2,0:T(8,128)S(1)} %multiply_bitcast_fusion), channel_id=1, replica_groups=mesh['dp'=2,'expert'=16] {'expert'}, dimensions={0}, use_global_device_ids=true | all-gather | bytes 34816 | tf_op jit(solution)/shard_map/all_gather | solution.py:67
  31.7 0.1 reshape.3
  31.9 30.9 %all-gather.3.cloned.1.call-done = bf16[512,4096]{1,0:T(8,128)(2,1)} async-done(((bf16[32,4096]{1,0:T(8,128)(2,1)}), bf16[512,4096]{1,0:T(8,128)(2,1)}) %all-gather.3.cloned.1.call-update) | async-done | bytes 4194320 | tf_op jit(solution)/shard_map/all_gather | solution.py:66
  62.8 7.0 %fusion.3 = f32[512,768]{1,0:T(8,128)S(1)} fusion(bf16[512,4096]{1,0:T(8,128)(2,1)} %all-gather.3.cloned.1.call-done, bf16[1,4096,768]{2,1,0:T(8,128)(2,1)} %param.9), kind=kOutput, calls=%fused_computation.4 | convolution fusion | flops 3221225472 | bytes 12058624 | tf_op jit(solution)/shard_map/dot_general | solution.py:69
  69.8 16.6 %multiply_convert_fusion = bf16[512,4096]{1,0:T(8,128)(2,1)} fusion(bf16[1,768,4096]{2,1,0:T(8,128)(2,1)} %param.11, f32[512]{0:T(512)S(1)} %bitcast.20, f32[512,768]{1,0:T(8,128)S(1)} %fusion.3, bf16[512,4096]{1,0:T(8,128)(2,1)} %all-gather.3.cloned.1.call-done, bf16[1,4096,768]{2,1,0:T(8,128)(2,1)} %param.10), kind=kOutput, calls=%fused_computation | convolution fusion | flops 6449004544 | bytes 22546432 | tf_op jit(solution)/shard_map/dot_general | solution.py:72
  86.4 0.0 reduce-scatter.2.cloned.1.call-update
  86.4 0.0 all-reduce.2.cloned.1.call-start
  86.5 71.4 %reduce-scatter.2.cloned.1.call-done = bf16[32,4096]{1,0:T(8,128)(2,1)} async-done(((bf16[512,4096]{1,0:T(8,128)(2,1)}), bf16[32,4096]{1,0:T(8,128)(2,1)}) %reduce-scatter.2.cloned.1.call-update) | async-done | bytes 262160 | tf_op jit(solution)/shard_map/reduce_scatter | solution.py:73
  157.9 0.0 all-reduce.2.cloned.1.call-update
  157.9 24.6 %all-reduce.2.cloned.1.call-done = bf16[32,4096]{1,0:T(8,128)(2,1)} async-done(((bf16[32,4096]{1,0:T(8,128)(2,1)}), bf16[32,4096]{1,0:T(8,128)(2,1)}) %all-reduce.2.cloned.1.call-update) | async-done | bytes 262160 | tf_op jit(solution)/shard_map/psum | solution.py:74
  182.5 1.7 copy.18
  (3 shorter events, 0.1 us)
Async XLA Ops:
  6.5 56.3 %all-gather.3.cloned.1.call-start = ((), (), s32[]{:S(2)}) async-start(), calls=%async_computation.1 | async-start | bytes 4456448 | tf_op jit(solution)/shard_map/all_gather | solution.py:66
  7.3 150.6 %reduce-scatter.2.cloned.1.call-start = ((), (), s32[]{:S(2)}) async-start(), calls=%async_computation.2 | async-start | bytes 4456448 | tf_op jit(solution)/shard_map/reduce_scatter | solution.py:73
  86.4 96.1 %all-reduce.2.cloned.1.call-start = ((), (), s32[]{:S(2)}) async-start(), calls=%async_computation.3 | async-start | bytes 524288 | tf_op jit(solution)/shard_map/psum | solution.py:74
Sparse Core Ops, SparseCore 0:
  9.5 53.2 all-gather.2
  86.6 71.2 reduce-scatter.1
  160.2 22.2 all-reduce.1
where the time goes:
time: 191 us
  waiting for transfers between devices  128 us (67%)
  blocking collectives  23.6 us (12%)
  matrix products  23.6 us (12%)
  between operations  13.1 us (7%)
    reduce_scatter x1, waiting for transfers between devices, dense_form(): lax.psum_scatter(part.astype(jnp.bfloat16), 'expert', scatter_dimension=0...  71.4 us
    all_gather x1, waiting for transfers between devices, dense_form(): rows = lax.all_gather(tokens, 'expert', axis=0, tiled=True)  30.9 us
    psum x1, waiting for transfers between devices, dense_form(): return lax.psum(local, 'dp')  24.6 us
    all_gather x1, blocking collectives, dense_form(): coefs = lax.all_gather(coef, 'expert', axis=0, tiled=True)  23.6 us
    dot_general x1, matrix products, dense_form(): part = mine * jnp.dot(hidden, w_down[0], preferred_element_type=jnp.float32)  16.6 us
    dot_general x1, matrix products, dense_form(): gate = jnp.dot(rows, w_gate[0], preferred_element_type=jnp.float32)  7.03 us
  transfers between devices with their start and end apart: 3, of which 3 were waited for; matrix products, arithmetic and copies ran while one was open for 0% of the time, Pallas kernels for 0%

commit v1 on v0

--- a/solution.py
+++ b/solution.py
@@ -63,8 +63,11 @@
     me = lax.axis_index("expert")
     chosen = expert_ids[:, :, None] == jnp.arange(groups, dtype=jnp.int32)[None, None, :]
     coef = jnp.sum(jnp.where(chosen, gate_ints[:, :, None], 0), axis=1).astype(jnp.float32) / 1024.0
-    rows = lax.all_gather(tokens, "expert", axis=0, tiled=True)
-    coefs = lax.all_gather(coef, "expert", axis=0, tiled=True)
+    rows, coefs = jnp.split(
+        lax.all_gather(jnp.concatenate([tokens, coef], axis=1), "expert", axis=0, tiled=True),
+        [tokens.shape[1]],
+        axis=1,
+    )
     mine = lax.dynamic_slice_in_dim(coefs, me, 1, axis=1)
     gate = jnp.dot(rows, w_gate[0], preferred_element_type=jnp.float32)
     up = jnp.dot(rows, w_up[0], preferred_element_type=jnp.float32)

time: 191 us -> 220 us (1.15)
  waiting for transfers between devices: 128 us -> 175 us
  blocking collectives: 23.6 us -> 0 us
    all_gather x1, waiting for transfers between devices: 30.9 us -> 79 us  [dense_form(): lax.all_gather(jnp.concatenate([tokens, coef], axis=1), 'expert', axis=0,...]
    all_gather x1 -> x0, blocking collectives: 23.6 us -> none  [dense_form(): coefs = lax.all_gather(coef, 'expert', axis=0, tiled=True)]
where the time goes in v1:
time: 220 us; the launch traced here: 219 us
  waiting for transfers between devices  175 us (80%)
  matrix products  25.5 us (12%)
  between operations  13.1 us (6%)
  local copies, waits for them, and re-layouts  2.95 us (1%)
  other arithmetic  2.59 us (1%)
    all_gather x1, waiting for transfers between devices, dense_form(): lax.all_gather(jnp.concatenate([tokens, coef], axis=1), 'expert', axis=0,...  79 us
    reduce_scatter x1, waiting for transfers between devices, dense_form(): lax.psum_scatter(part.astype(jnp.bfloat16), 'expert', scatter_dimension=0...  71.4 us
    psum x1, waiting for transfers between devices, dense_form(): return lax.psum(local, 'dp')  24.6 us
    dot_general x1, matrix products, dense_form(): part = mine * jnp.dot(hidden, w_down[0], preferred_element_type=jnp.float32)  17.8 us
    dot_general x1, matrix products, dense_form(): gate = jnp.dot(rows, w_gate[0], preferred_element_type=jnp.float32)  7.68 us
  transfers between devices with their start and end apart: 3, of which 3 were waited for; matrix products, arithmetic and copies ran while one was open for 0% of the time, Pallas kernels for 0%

profile of v1, /device:TPU:0, one launch (start us, length us, event | category | flops | bytes accessed | tf_op | source)
XLA Modules:
  0.0 219.3 jit_solution(799332968160529200)
XLA Ops:
  6.5 0.0 all-gather.2.cloned.1.call-start
  6.5 0.7 select_reduce_fusion
  7.3 0.1 copy.11
  7.3 1.0 convert_element_type.12
  8.3 0.9 pad_maximum_fusion
  9.2 0.0 all-gather.2.cloned.1.call-update
  9.2 0.0 reduce-scatter.2.cloned.1.call-start
  9.3 79.0 %all-gather.2.cloned.1.call-done = f32[512,4112]{1,0:T(8,128)} async-done(((f32[32,4112]{1,0:T(8,128)}), f32[512,4112]{1,0:T(8,128)}) %all-gather.2.cloned.1.call-update) | async-done | bytes 8421392 | tf_op jit(solution)/shard_map/all_gather | solution.py:67
  88.3 1.0 split.8
  89.3 0.2 dynamic-slice_reduce_fusion
  89.5 7.7 %fusion.2 = f32[512,768]{1,0:T(8,128)S(1)} fusion(f32[512,4112]{1,0:T(8,128)} %all-gather.2.cloned.1.call-done, bf16[1,4096,768]{2,1,0:T(8,128)(2,1)} %param.9), kind=kOutput, calls=%fused_computation.3 | convolution fusion | flops 3221225472 | bytes 12058624 | tf_op jit(solution)/shard_map/dot_general | solution.py:72
  97.2 17.8 %multiply_convert_fusion = bf16[512,4096]{1,0:T(8,128)(2,1)} fusion(bf16[1,768,4096]{2,1,0:T(8,128)(2,1)} %param.11, f32[512]{0:T(512)S(1)} %dynamic-slice_reduce_fusion, f32[512,768]{1,0:T(8,128)S(1)} %fusion.2, bf16[1,4096,768]{2,1,0:T(8,128)(2,1)} %param.10, f32[512,4112]{1,0:T(8,128)} %all-gather.2.cloned.1.call-done), kind=kOutput, calls=%fused_computation | convolution fusion | flops 6449004544 | bytes 22546432 | tf_op jit(solution)/shard_map/dot_general | solution.py:75
  115.0 0.0 reduce-scatter.2.cloned.1.call-update
  115.0 0.0 all-reduce.2.cloned.1.call-start
  115.1 71.4 %reduce-scatter.2.cloned.1.call-done = bf16[32,4096]{1,0:T(8,128)(2,1)} async-done(((bf16[512,4096]{1,0:T(8,128)(2,1)}), bf16[32,4096]{1,0:T(8,128)(2,1)}) %reduce-scatter.2.cloned.1.call-update) | async-done | bytes 262160 | tf_op jit(solution)/shard_map/reduce_scatter | solution.py:76
  186.5 0.0 all-reduce.2.cloned.1.call-update
  186.5 24.6 %all-reduce.2.cloned.1.call-done = bf16[32,4096]{1,0:T(8,128)(2,1)} async-done(((bf16[32,4096]{1,0:T(8,128)(2,1)}), bf16[32,4096]{1,0:T(8,128)(2,1)}) %all-reduce.2.cloned.1.call-update) | async-done | bytes 262160 | tf_op jit(solution)/shard_map/psum | solution.py:77
  211.1 1.7 copy.13
  (1 shorter events, 0.0 us)
Async XLA Ops:
  6.5 81.8 %all-gather.2.cloned.1.call-start = ((), (), s32[]{:S(2)}) async-start(), calls=%async_computation.1 | async-start | bytes 9191424 | tf_op jit(solution)/shard_map/all_gather | solution.py:67
  9.2 177.3 %reduce-scatter.2.cloned.1.call-start = ((), (), s32[]{:S(2)}) async-start(), calls=%async_computation.2 | async-start | bytes 4456448 | tf_op jit(solution)/shard_map/reduce_scatter | solution.py:76
  115.0 96.1 %all-reduce.2.cloned.1.call-start = ((), (), s32[]{:S(2)}) async-start(), calls=%async_computation.3 | async-start | bytes 524288 | tf_op jit(solution)/shard_map/psum | solution.py:77
Sparse Core Ops, SparseCore 0:
  9.6 78.6 all-gather.1
  115.1 71.2 reduce-scatter.1
  188.8 22.3 all-reduce.1

commit v2 on v0

--- a/solution.py
+++ b/solution.py
@@ -71,7 +71,7 @@
     hidden = (jax.nn.silu(gate) * up).astype(jnp.bfloat16)
     part = mine * jnp.dot(hidden, w_down[0], preferred_element_type=jnp.float32)
     local = lax.psum_scatter(part.astype(jnp.bfloat16), "expert", scatter_dimension=0, tiled=True)
-    return lax.psum(local, "dp")
+    return jnp.sum(lax.all_gather(local, "dp"), axis=0)
 
 
 def on_device(tokens, expert_ids, *rest):

time: 191 us -> 173 us (0.906)
  waiting for transfers between devices: 128 us -> 103 us
  blocking collectives: 23.6 us -> 31 us
    psum x1 -> x0, waiting for transfers between devices: 24.6 us -> none  [dense_form(): return lax.psum(local, 'dp')]
    all_gather x0 -> x1, blocking collectives: none -> 7.39 us  [dense_form(): return jnp.sum(lax.all_gather(local, 'dp'), axis=0)]
  transfers between devices with their start and end apart: 3 -> 2, of which waited for: 3 -> 2; matrix products, arithmetic and copies ran while one was open for 0% -> 1% of each run, Pallas kernels for 0% -> 0%
where the time goes in v2:
time: 173 us
  waiting for transfers between devices  103 us (60%)
  blocking collectives  31 us (18%)
  matrix products  23.6 us (14%)
  between operations  13.4 us (8%)
    reduce_scatter x1, waiting for transfers between devices, dense_form(): lax.psum_scatter(part.astype(jnp.bfloat16), 'expert', scatter_dimension=0...  71.5 us
    all_gather x1, waiting for transfers between devices, dense_form(): rows = lax.all_gather(tokens, 'expert', axis=0, tiled=True)  30.9 us
    all_gather x1, blocking collectives, dense_form(): coefs = lax.all_gather(coef, 'expert', axis=0, tiled=True)  23.6 us
    dot_general x1, matrix products, dense_form(): part = mine * jnp.dot(hidden, w_down[0], preferred_element_type=jnp.float32)  16.6 us
    all_gather x1, blocking collectives, dense_form(): return jnp.sum(lax.all_gather(local, 'dp'), axis=0)  7.39 us
    dot_general x1, matrix products, dense_form(): gate = jnp.dot(rows, w_gate[0], preferred_element_type=jnp.float32)  7.03 us
  transfers between devices with their start and end apart: 2, of which 2 were waited for; matrix products, arithmetic and copies ran while one was open for 1% of the time, Pallas kernels for 0%

profile of v2, /device:TPU:0, one launch (start us, length us, event | category | flops | bytes accessed | tf_op | source)
XLA Modules:
  0.0 173.0 jit_solution(10782803829590468985)
XLA Ops:
  6.5 0.0 all-gather.4.cloned.1.call-start
  6.5 0.7 all-gather.4.cloned.1.call-update
  7.3 0.0 reduce-scatter.2.cloned.1.call-start
  7.3 0.7 select_reduce_fusion
  8.0 23.6 %all-gather.1 = f32[16,32,16]{1,2,0:T(8,128)S(1)} all-gather(f32[1,32,16]{1,2,0:T(8,128)S(1)} %multiply_bitcast_fusion), channel_id=1, replica_groups=mesh['dp'=2,'expert'=16] {'expert'}, dimensions={0}, use_global_device_ids=true | all-gather | bytes 34816 | tf_op jit(solution)/shard_map/all_gather | solution.py:67
  31.7 0.1 reshape.4
  31.9 30.9 %all-gather.4.cloned.1.call-done = bf16[512,4096]{1,0:T(8,128)(2,1)} async-done(((bf16[32,4096]{1,0:T(8,128)(2,1)}), bf16[512,4096]{1,0:T(8,128)(2,1)}) %all-gather.4.cloned.1.call-update) | async-done | bytes 4194320 | tf_op jit(solution)/shard_map/all_gather | solution.py:66
  62.8 7.0 %fusion.3 = f32[512,768]{1,0:T(8,128)S(1)} fusion(bf16[512,4096]{1,0:T(8,128)(2,1)} %all-gather.4.cloned.1.call-done, bf16[1,4096,768]{2,1,0:T(8,128)(2,1)} %param.9), kind=kOutput, calls=%fused_computation.4 | convolution fusion | flops 3221225472 | bytes 12058624 | tf_op jit(solution)/shard_map/dot_general | solution.py:69
  69.8 16.6 %multiply_convert_fusion = bf16[512,4096]{1,0:T(8,128)(2,1)} fusion(bf16[1,768,4096]{2,1,0:T(8,128)(2,1)} %param.11, f32[512]{0:T(512)S(1)} %bitcast.22, f32[512,768]{1,0:T(8,128)S(1)} %fusion.3, bf16[512,4096]{1,0:T(8,128)(2,1)} %all-gather.4.cloned.1.call-done, bf16[1,4096,768]{2,1,0:T(8,128)(2,1)} %param.10), kind=kOutput, calls=%fused_computation | convolution fusion | flops 6449004544 | bytes 22546432 | tf_op jit(solution)/shard_map/dot_general | solution.py:72
  86.4 0.0 reduce-scatter.2.cloned.1.call-update
  86.4 71.5 %reduce-scatter.2.cloned.1.call-done = bf16[32,4096]{1,0:T(8,128)(2,1)} async-done(((bf16[512,4096]{1,0:T(8,128)(2,1)}), bf16[32,4096]{1,0:T(8,128)(2,1)}) %reduce-scatter.2.cloned.1.call-update) | async-done | bytes 262160 | tf_op jit(solution)/shard_map/reduce_scatter | solution.py:73
  157.9 7.4 %all-gather = bf16[64,4096]{1,0:T(8,128)(2,1)S(1)} all-gather(bf16[32,4096]{1,0:T(8,128)(2,1)} %reduce-scatter.2.cloned.1.call-done), channel_id=2, replica_groups=mesh['dp'=2,'expert'=16] {'dp'}, dimensions={0}, use_global_device_ids=true | all-gather | bytes 786432 | tf_op jit(solution)/shard_map/all_gather | solution.py:74
  165.3 0.8 reduce_sum.22
  (3 shorter events, 0.1 us)
Async XLA Ops:
  6.5 56.3 %all-gather.4.cloned.1.call-start = ((), (), s32[]{:S(2)}) async-start(), calls=%async_computation.1 | async-start | bytes 4456448 | tf_op jit(solution)/shard_map/all_gather | solution.py:66
  7.3 150.6 %reduce-scatter.2.cloned.1.call-start = ((), (), s32[]{:S(2)}) async-start(), calls=%async_computation.2 | async-start | bytes 4456448 | tf_op jit(solution)/shard_map/reduce_scatter | solution.py:73
Sparse Core Ops, SparseCore 0:
  9.5 53.2 all-gather.3
  86.5 71.2 reduce-scatter.1
